TPU v7x, 32 devices: a whole 2x2x4 slice. The times are simulated.
32 devices in a mesh: dp: 4 (over x, core), expert: 8 (over z, y).
Axes of the slice: x: 2, y: 2, z: 4, core: 2. Of those that a mesh axis runs over, the one named last changes fastest.
Arguments:
- tokens: bfloat16 [4096, 2048], P(('dp', 'expert')), may hold values from -6 to 6
- expert_ids: int32 [4096, 8], P(('dp', 'expert')), may hold values from 0 to 127, all different within a row; in each aligned block of 128 rows (0 to 127, 128 to 255, ...) at most 20 rows name the same one
- gate_probs: float32 [4096, 8], P(('dp', 'expert')), may hold values from 0.05 to 1
- gate_weight: bfloat16 [128, 768, 2048], P(('dp', 'expert')), may hold values from -0.125 to 0.125
- up_weight: bfloat16 [128, 768, 2048], P(('dp', 'expert')), may hold values from -0.125 to 0.125
- down_weight: bfloat16 [128, 768, 2048], P(('dp', 'expert')), may hold values from -0.4375 to 0.4375
Outputs:
- mixed: bfloat16 [4096, 2048], P(('dp', 'expert'))
- expert_load: float32 [128], replicated
Inputs may be any that keep to these rules, and one draw needn't show every extreme that they name: `expert_ids`: in each block of 128 consecutive tokens no expert is named by more than 20 pairs, a bound that some blocks reach; every expert is named somewhere.
All inputs are finite; a program needn't handle non-finite values.
Results may differ from a plain program's by a relative error of at most 0.0085.
Values may be sent and summed in bfloat16 or wider, within the bound.
A program may use at most 128 MiB of HBM per device.

v0:
```python
import jax
import jax.numpy as jnp
from jax import lax
from jax.sharding import PartitionSpec as P

CAP = 20


def expert_block(arrived, gate_weight, up_weight, down_weight):
    gate_part = jnp.einsum(
        "sekd,efd->sekf", arrived, gate_weight, preferred_element_type=jnp.float32
    )
    up_part = jnp.einsum("sekd,efd->sekf", arrived, up_weight, preferred_element_type=jnp.float32)
    hidden = (jax.nn.silu(gate_part) * up_part).astype(jnp.bfloat16)
    produced = jnp.einsum("sekf,efd->sekd", hidden, down_weight, preferred_element_type=jnp.float32)
    return produced.astype(jnp.bfloat16)


def on_device(tokens, expert_ids, gate_probs, gate_weight, up_weight, down_weight):
    tok_rows, features = tokens.shape
    chosen = expert_ids.shape[1]
    owned = gate_weight.shape[0]
    devices = lax.axis_size(("dp", "expert"))
    experts = owned * devices
    pairs = tok_rows * chosen
    flat_ids = expert_ids.reshape(pairs)
    one_hot = (flat_ids[:, None] == lax.iota(jnp.int32, experts)[None, :]).astype(jnp.int32)
    earlier = jnp.cumsum(one_hot, axis=0) - one_hot
    slot_index = jnp.sum(earlier * one_hot, axis=1)
    target = flat_ids * CAP + slot_index
    owner_row = lax.iota(jnp.int32, pairs) // chosen
    source_row = jnp.full((experts * CAP,), tok_rows, jnp.int32).at[target].set(owner_row)
    padded = jnp.concatenate([tokens, jnp.zeros((1, features), tokens.dtype)], axis=0)
    outgoing = padded[source_row].reshape(devices, owned, CAP, features)
    counts = lax.psum(jnp.sum(one_hot, axis=0).astype(jnp.float32), ("dp", "expert"))
    produced = expert_block(
        lax.all_to_all(outgoing, ("dp", "expert"), split_axis=0, concat_axis=0, tiled=True),
        gate_weight,
        up_weight,
        down_weight,
    )
    returned = lax.all_to_all(produced, ("dp", "expert"), split_axis=0, concat_axis=0, tiled=True)
    results = returned.reshape(experts * CAP, features)
    picked = results[target].reshape(tok_rows, chosen, features)
    weights = gate_probs / jnp.sum(gate_probs, axis=1, keepdims=True)
    mixed = jnp.einsum("tk,tkd->td", weights, picked.astype(jnp.float32)).astype(jnp.bfloat16)
    expert_load = counts * (experts / (tok_rows * devices * chosen))
    return (mixed, expert_load)


def solution(mesh):
    in_specs = (
        P(("dp", "expert"), None),
        P(("dp", "expert"), None),
        P(("dp", "expert"), None),
        P(("dp", "expert"), None, None),
        P(("dp", "expert"), None, None),
        P(("dp", "expert"), None, None),
    )
    out_specs = (P(("dp", "expert"), None), P())
    return jax.shard_map(
        on_device, mesh=mesh, in_specs=in_specs, out_specs=out_specs, check_vma=False
    )
```

profile of v0, /device:TPU:0, one launch (start us, length us, event | category | flops | bytes accessed | tf_op | source)
XLA Modules:
  0.0 692.8 jit_solution(644135197542510640)
XLA Ops:
  0.6 0.8 copy.24
  1.4 0.1 eq.29
  1.5 0.1 eq.25
  1.6 0.7 broadcast_multiply_fusion
  2.3 0.1 copy.26
  2.4 0.2 fusion.22
  2.7 0.1 copy.27
  2.8 0.1 copy.23
  2.9 0.1 mul.34
  3.0 0.4 convert_reduce_fusion
  3.4 4.3 scatter_custom_fusion
  7.7 1.1 concatenate.3
  8.8 10.9 %gather_fusion = bf16[2560,2048]{1,0:T(8,128)(2,1)} fusion(bf16[129,2048]{1,0:T(8,128)(2,1)S(1)} %concatenate.3, s32[3072]{0:T(1024)S(1)} %pad_clamp_fusion), kind=kCustom, calls=%fused_computation | custom fusion | bytes 20981760 | tf_op jit(solution)/shard_map/gather | solution.py:34
  19.7 16.4 %reshape.61 = bf16[32,4,20,2048]{3,2,1,0:T(8,128)(2,1)} reshape(bf16[2560,2048]{1,0:T(8,128)(2,1)} %gather_fusion) | data formatting | bytes 20971520 | tf_op jit(solution)/shard_map/reshape | solution.py:34
  36.1 12.8 %copy.28 = bf16[32,4,20,2048]{3,1,2,0:T(4,128)(2,1)S(1)} copy(bf16[32,4,20,2048]{3,2,1,0:T(8,128)(2,1)} %reshape.61) | data formatting | bytes 20971520 | tf_op jit(solution)/shard_map/reshape | solution.py:34
  48.9 237.2 %all_to_all.10 = bf16[32,4,20,2048]{3,1,2,0:T(4,128)(2,1)} all-to-all(bf16[32,4,20,2048]{3,1,2,0:T(4,128)(2,1)S(1)} %copy.28), channel_id=1, replica_groups=mesh['dp'=4,'expert'=8] {'dp','expert'}, dimensions={0} | all-to-all | bytes 20971520 | tf_op jit(solution)/shard_map/all_to_all | solution.py:37
  286.1 27.2 %fusion.2 = f32[4,32,20,768]{3,1,2,0:T(8,128)} fusion(bf16[4,768,2048]{2,1,0:T(8,128)(2,1)} %param.10, bf16[32,4,20,2048]{3,1,2,0:T(4,128)(2,1)} %all_to_all.10), kind=kOutput, calls=%fused_computation.5 | convolution fusion | flops 8053063680 | bytes 30932992 | tf_op jit(solution)/shard_map/sekd,efd->sekf/dot_general | solution.py:13
  313.2 33.0 %fusion.8 = bf16[32,4,20,768]{3,0,2,1:T(8,128)(2,1)} fusion(f32[4,32,20,768]{3,1,2,0:T(8,128)} %fusion.2, bf16[4,768,2048]{2,1,0:T(8,128)(2,1)} %param.9, bf16[32,4,20,2048]{3,1,2,0:T(4,128)(2,1)} %all_to_all.10), kind=kOutput, calls=%fused_computation.13 | convolution fusion | flops 8064860160 | bytes 34865152 | tf_op jit(solution)/shard_map/sekd,efd->sekf/dot_general | solution.py:10
  346.2 13.9 %convert_bitcast_fusion = bf16[32,4,20,2048]{3,0,2,1:T(8,128)(2,1)S(1)} fusion(bf16[32,4,20,768]{3,0,2,1:T(8,128)(2,1)} %fusion.8, bf16[4,768,2048]{2,1,0:T(8,128)(2,1)} %param.11), kind=kOutput, calls=%fused_computation.9 | convolution fusion | flops 8058306560 | bytes 27000832 | tf_op jit(solution)/shard_map/sekf,efd->sekd/dot_general | solution.py:15
  360.1 24.1 %copy.31 = bf16[32,4,20,2048]{3,1,2,0:T(4,128)(2,1)} copy(bf16[32,4,20,2048]{3,0,2,1:T(8,128)(2,1)S(1)} %convert_bitcast_fusion) | data formatting | bytes 20971520 | tf_op jit(solution)/shard_map/convert_element_type | solution.py:16
  384.2 0.0 copy-start
  384.2 3.9 all-to-all-start.1
  388.1 0.0 copy-done
  388.1 0.1 copy.36
  388.2 254.7 %psum.7 = f32[128]{0:T(128)S(1)} all-reduce(f32[128]{0:T(128)S(1)} %convert_element_type.29), channel_id=1, replica_groups=mesh['dp'=4,'expert'=8] {'dp','expert'}, use_global_device_ids=true, to_apply=%region_6.7 | all-reduce | flops 128 | bytes 1024 | tf_op jit(solution)/shard_map/psum | solution.py:35
  642.9 0.5 broadcast_multiply_fusion.1
  643.4 0.0 all-to-all-done.1
  643.4 14.0 %copy.32 = bf16[32,4,20,2048]{3,2,1,0:T(8,128)(2,1)} copy(bf16[32,4,20,2048]{3,1,2,0:T(4,128)(2,1)} %all-to-all-done.1) | data formatting | bytes 20971520 | tf_op jit(solution)/shard_map/all_to_all | solution.py:42
  657.4 16.5 %reshape.62 = bf16[2560,2048]{1,0:T(8,128)(2,1)} reshape(bf16[32,4,20,2048]{3,2,1,0:T(8,128)(2,1)} %copy.32) | data formatting | bytes 20971520 | tf_op jit(solution)/shard_map/reshape | solution.py:43
  673.9 14.2 %gather_fusion.1 = bf16[1024,2048]{1,0:T(8,128)(2,1)} fusion(bf16[2560,2048]{1,0:T(8,128)(2,1)} %reshape.62, s32[1024]{0:T(1024)S(1)} %broadcast_clamp_fusion), kind=kCustom, calls=%fused_computation.1 | custom fusion | bytes 8392704 | tf_op jit(solution)/shard_map/gather | solution.py:44
  688.1 3.4 fusion.18
  691.5 1.1 copy.45
  (12 shorter events, 0.1 us)
Async XLA Ops:
  384.2 3.9 copy-start
  384.2 259.3 %all-to-all-start.1 = ((bf16[32,4,20,2048]{3,1,2,0:T(4,128)(2,1)}), bf16[32,4,20,2048]{3,1,2,0:T(4,128)(2,1)}, u32[]{:S(2)}, u32[]{:S(2)}) async-start(bf16[32,4,20,2048]{3,1,2,0:T(4,128)(2,1)} %copy.31), calls=%async_computation.1 | async-start | bytes 20971520 | tf_op jit(solution)/shard_map/all_to_all | solution.py:42
where the time goes:
time: 698 us; the launch traced here: 693 us
  blocking collectives  492 us (70%)
  local copies, waits for them, and re-layouts  117 us (17%)
  matrix products  77.4 us (11%)
    psum x1, blocking collectives, on_device(): lax.psum(jnp.sum(one_hot, axis=0).astype(jnp.float32), ('dp', 'expert'))  255 us
    all_to_all x1, blocking collectives, on_device(): lax.all_to_all(outgoing, ('dp', 'expert'), split_axis=0, concat_axis=0, t...  237 us
    dot_general x1, matrix products, expert_block(): jnp.einsum('sekd,efd->sekf', arrived, gate_weight, preferred_element_type...  33 us
    reshape x2, local copies, waits for them, and re-layouts, on_device(): outgoing = padded[source_row].reshape(devices, owned, CAP, features)  29.1 us
    dot_general x1, matrix products, expert_block(): jnp.einsum('sekd,efd->sekf', arrived, up_weight, preferred_element_type=j...  27.2 us
    convert_element_type x1, local copies, waits for them, and re-layouts, expert_block(): return produced.astype(jnp.bfloat16)  24.1 us
    reshape x1, local copies, waits for them, and re-layouts, on_device(): results = returned.reshape(experts * CAP, features)  16.5 us
    gather x1, local copies, waits for them, and re-layouts, on_device(): picked = results[target].reshape(tok_rows, chosen, features)  14.2 us
  transfers between devices with their start and end apart: 1, of which 0 were waited for; matrix products, arithmetic and copies ran while one was open for 0% of the time, Pallas kernels for 0%

commit v1 on v0

v1 whole, which is shorter than its diff:
```python
import jax
import jax.numpy as jnp
from jax import lax
from jax.sharding import PartitionSpec as P

CAP = 20
AXES = ("dp", "expert")
CHUNKS = 2


def on_device(tokens, expert_ids, gate_probs, gate_weight, up_weight, down_weight):
    rows, features = tokens.shape
    top = expert_ids.shape[1]
    owned = gate_weight.shape[0]
    devices = lax.axis_size(AXES)
    me = lax.axis_index(AXES)
    experts = owned * devices
    bf16, f32 = jnp.bfloat16, jnp.float32
    cut = features // CHUNKS

    weights = gate_probs / jnp.sum(gate_probs, axis=1, keepdims=True)
    every = lax.iota(jnp.int32, experts)
    named = (expert_ids.reshape(rows * top)[:, None] == every[None, :]).astype(f32)
    counts = jnp.sum(named, axis=0)
    meta = jnp.concatenate(
        [expert_ids.astype(f32).reshape(-1), weights.reshape(-1), counts]
    )
    meta = lax.all_gather(meta.reshape(1, -1), AXES, axis=0, tiled=True)
    arriving = [
        lax.all_gather(tokens[:, c * cut : (c + 1) * cut], AXES, axis=0, tiled=True)
        for c in range(CHUNKS)
    ]
    pairs = rows * top
    ids_all = meta[:, :pairs].reshape(devices, rows, top).astype(jnp.int32)
    w_all = meta[:, pairs : 2 * pairs].reshape(devices, rows, top)
    expert_load = jnp.sum(meta[:, 2 * pairs :], axis=0) * (experts / (rows * devices * top))

    mine = me * owned + lax.iota(jnp.int32, owned)
    hit = (ids_all[:, None, :, :] == mine[None, :, None, None]).astype(f32)
    chosen = jnp.sum(hit, axis=3)
    share = jnp.sum(hit * w_all[:, None, :, :], axis=3)
    before = (lax.iota(jnp.int32, rows)[:, None] < lax.iota(jnp.int32, rows)[None, :]).astype(bf16)
    slot = jnp.einsum("bet,tu->beu", chosen.astype(bf16), before, preferred_element_type=f32)
    slot = jnp.where(chosen > 0, slot, -1.0)
    pick = slot[:, :, None, :] == lax.iota(jnp.int32, CAP).astype(f32)[None, None, :, None]
    scale = jnp.sum(jnp.where(pick, share[:, :, None, :], 0.0), axis=3)
    pick = pick.astype(bf16)

    gate = up = 0.0
    for c in range(CHUNKS):
        block = arriving[c].reshape(devices, rows, cut)
        x = jnp.einsum("best,btd->ebsd", pick, block, preferred_element_type=f32)
        x = x.astype(bf16).reshape(owned, devices * CAP, cut)
        span = slice(c * cut, (c + 1) * cut)
        gate += jnp.einsum("ekd,efd->ekf", x, gate_weight[:, :, span], preferred_element_type=f32)
        up += jnp.einsum("ekd,efd->ekf", x, up_weight[:, :, span], preferred_element_type=f32)
    hidden = (jax.nn.silu(gate) * up).astype(bf16)
    scale = scale.transpose(1, 0, 2).reshape(owned, devices * CAP, 1)
    mixed = []
    for c in range(CHUNKS):
        span = slice(c * cut, (c + 1) * cut)
        y = jnp.einsum("ekf,efd->ekd", hidden, down_weight[:, :, span], preferred_element_type=f32)
        y = (y * scale).astype(bf16).reshape(owned, devices, CAP, cut)
        part = jnp.einsum("best,ebsd->btd", pick, y, preferred_element_type=f32)
        part = part.astype(bf16).reshape(devices * rows, cut)
        mixed.append(lax.psum_scatter(part, AXES, scatter_dimension=0, tiled=True))
    return jnp.concatenate(mixed, axis=1), expert_load


def solution(mesh):
    in_specs = (
        P(AXES, None),
        P(AXES, None),
        P(AXES, None),
        P(AXES, None, None),
        P(AXES, None, None),
        P(AXES, None, None),
    )
    return jax.shard_map(
        on_device, mesh=mesh, in_specs=in_specs, out_specs=(P(AXES, None), P()), check_vma=False
    )
```

time: 698 us -> 618 us (0.89)
  blocking collectives: 492 us -> 73.1 us
  waiting for transfers between devices: 0.01 us -> 403 us
  local copies, waits for them, and re-layouts: 117 us -> 24.4 us
  between operations: 0.99 us -> 14.2 us
  matrix products: 77.4 us -> 89.9 us
    reduce_scatter x0 -> x2, waiting for transfers between devices: none -> 351 us  [on_device(): mixed.append(lax.psum_scatter(part, AXES, scatter_dimension=0, tiled=True))]
    psum x1 -> x0, blocking collectives: 255 us -> none  [on_device(): lax.psum(jnp.sum(one_hot, axis=0).astype(jnp.float32), ('dp', 'expert'))]
    all_to_all x1 -> x0, blocking collectives: 237 us -> none  [on_device(): lax.all_to_all(outgoing, ('dp', 'expert'), split_axis=0, concat_axis=0, t...]
    all_gather x0 -> x1, blocking collectives: none -> 73.1 us  [on_device(): meta = lax.all_gather(meta.reshape(1, -1), AXES, axis=0, tiled=True)]
    all_gather x0 -> x2, waiting for transfers between devices: none -> 51.6 us  [on_device(): lax.all_gather(tokens[:, c * cut:(c + 1) * cut], AXES, axis=0, tiled=True)]
    reshape x3 -> x2, local copies, waits for them, and re-layouts: 45.6 us -> 0.18 us  [the longest x1 0.09 us: on_device(): weights.reshape(-1)]
    gather x2 -> x0, local copies, waits for them, and re-layouts: 25 us -> none  [the longest x1 14.2 us: on_device(): picked = results[target].reshape(tok_rows, chosen, features)]
    all_to_all x1 -> x0, local copies, waits for them, and re-layouts: 14 us -> none  [on_device(): lax.all_to_all(produced, ('dp', 'expert'), split_axis=0, concat_axis=0, t...]
  transfers between devices with their start and end apart: 1 -> 4, of which waited for: 0 -> 4; matrix products, arithmetic and copies ran while one was open for 0% -> 9% of each run, Pallas kernels for 0% -> 0%
where the time goes in v1:
time: 618 us; the launch traced here: 611 us
  waiting for transfers between devices  403 us (65%)
  matrix products  89.9 us (15%)
  blocking collectives  73.1 us (12%)
  local copies, waits for them, and re-layouts  24.4 us (4%)
  between operations  14.2 us (2%)
    reduce_scatter x2, waiting for transfers between devices, on_device(): mixed.append(lax.psum_scatter(part, AXES, scatter_dimension=0, tiled=True))  351 us
    all_gather x1, blocking collectives, on_device(): meta = lax.all_gather(meta.reshape(1, -1), AXES, axis=0, tiled=True)  73.1 us
    all_gather x2, waiting for transfers between devices, on_device(): lax.all_gather(tokens[:, c * cut:(c + 1) * cut], AXES, axis=0, tiled=True)  51.6 us
    dot_general x2, matrix products, on_device(): jnp.einsum('ekd,efd->ekf', x, gate_weight[:, :, span], preferred_element_...  30.9 us
    dot_general x2, matrix products, on_device(): jnp.einsum('ekd,efd->ekf', x, up_weight[:, :, span], preferred_element_ty...  20.5 us
    dot_general x2, matrix products, on_device(): jnp.einsum('ekf,efd->ekd', hidden, down_weight[:, :, span], preferred_ele...  16.4 us
  transfers between devices with their start and end apart: 4, of which 4 were waited for; matrix products, arithmetic and copies ran while one was open for 9% of the time, Pallas kernels for 0%

profile of v1, /device:TPU:0, one launch (start us, length us, event | category | flops | bytes accessed | tf_op | source)
XLA Modules:
  0.0 610.8 jit_solution(2428310687486948483)
XLA Ops:
  7.2 0.0 all-gather.7.cloned.1.call-start
  7.2 1.9 fusion.44
  9.1 0.0 all-gather.7.cloned.1.call-update
  9.1 0.0 all-gather.5.cloned.1.call-start
  9.1 0.7 all-gather.5.cloned.1.call-update
  9.8 0.0 reduce-scatter.3.cloned.1.call-start
  9.9 0.7 convert_element_type.58
  10.6 0.8 copy.66
  11.4 0.7 reduce_sum.54
  12.1 0.7 broadcast_divide_fusion
  12.8 0.1 copy.65
  12.9 0.1 reshape.60
  13.0 0.1 copy.64
  13.1 0.1 reshape.59
  13.2 0.1 eq.20
  13.2 0.2 convert_reduce_fusion
  13.5 73.1 %all-gather.1 = f32[32,1,2176]{2,1,0:T(1,128)S(1)} all-gather(f32[1,1,2176]{2,1,0:T(1,128)S(1)} %reshape.71), channel_id=2, replica_groups=mesh['dp'=4,'expert'=8] {'dp','expert'}, dimensions={0}, use_global_device_ids=true | all-gather | bytes 287232 | tf_op jit(solution)/shard_map/all_gather | solution.py:28
  86.7 0.2 copy.67
  86.9 0.2 copy.68
  87.1 0.2 copy.78
  87.3 0.2 copy.79
  87.6 0.4 fusion.39
  88.0 0.1 convolution_select_fusion
  88.2 0.6 fusion.26
  88.9 0.1 mul.52
  89.0 3.6 all-gather.7.cloned.1.call-done
  92.6 5.2 convert_bitcast_fusion
  97.8 4.9 copy.74
  102.7 10.8 %fusion.10 = f32[4,640,768]{2,1,0:T(8,128)} fusion(bf16[4,768,2048]{2,1,0:T(8,128)(2,1)} %param.9, bf16[4,640,1024]{2,0,1:T(4,128)(2,1)S(1)} %bitcast.47), kind=kOutput, calls=%fused_computation.15 | convolution fusion | flops 4026531840 | bytes 19398656 | tf_op jit(solution)/shard_map/ekd,efd->ekf/dot_general | solution.py:55
  113.5 10.2 %fusion.6 = f32[4,640,768]{2,1,0:T(8,128)} fusion(bf16[4,768,2048]{2,1,0:T(8,128)(2,1)} %param.10, bf16[4,640,1024]{2,0,1:T(4,128)(2,1)S(1)} %bitcast.48), kind=kOutput, calls=%fused_computation.11 | convolution fusion | flops 4026531840 | bytes 19398656 | tf_op jit(solution)/shard_map/ekd,efd->ekf/dot_general | solution.py:56
  123.7 48.0 %all-gather.5.cloned.1.call-done = bf16[4096,1024]{1,0:T(8,128)(2,1)} async-done(((bf16[128,1024]{1,0:T(8,128)(2,1)}), bf16[4096,1024]{1,0:T(8,128)(2,1)}) %all-gather.5.cloned.1.call-update) | async-done | bytes 8388624 | tf_op jit(solution)/shard_map/all_gather | solution.py:30
  171.8 5.2 convert_bitcast_fusion.1
  177.0 4.9 copy.72
  181.9 0.0 copy-start
  181.9 2.4 copy-done
  184.2 10.3 %fusion.8 = f32[4,640,768]{2,1,0:T(8,128)} fusion(bf16[4,768,2048]{2,1,0:T(8,128)(2,1)} %param.10, bf16[4,640,1024]{2,0,1:T(4,128)(2,1)S(1)} %bitcast.45), kind=kOutput, calls=%fused_computation.13 | convolution fusion | flops 4026531840 | bytes 19398656 | tf_op jit(solution)/shard_map/ekd,efd->ekf/dot_general | solution.py:56
  194.5 20.1 %multiply_convert_fusion.2 = bf16[4,640,768]{2,1,0:T(8,128)(2,1)} fusion(f32[4,640,768]{2,1,0:T(8,128)} %fusion.8, f32[4,640,768]{2,1,0:T(8,128)} %fusion.6, f32[4,640,768]{2,1,0:T(8,128)} %fusion.10, bf16[4,768,2048]{2,1,0:T(8,128)(2,1)} %param.9, bf16[4,640,1024]{2,0,1:T(4,128)(2,1)} %bitcast.46), kind=kOutput, calls=%fused_computation.4 | convolution fusion | flops 4042260480 | bytes 39059456 | tf_op jit(solution)/shard_map/ekd,efd->ekf/dot_general | solution.py:55
  214.6 8.2 %multiply_convert_fusion.1 = bf16[4,640,1024]{2,1,0:T(8,128)(2,1)S(1)} fusion(f32[4,640]{1,0:T(4,128)S(1)} %mul.52, bf16[4,640,768]{2,1,0:T(8,128)(2,1)} %multiply_convert_fusion.2, bf16[4,768,2048]{2,1,0:T(8,128)(2,1)} %param.11), kind=kOutput, calls=%fused_computation.3 | convolution fusion | flops 4031774720 | bytes 15476736 | tf_op jit(solution)/shard_map/ekf,efd->ekd/dot_general | solution.py:62
  222.8 4.0 copy.81
  226.9 5.7 bitcast_convert_fusion.1
  232.6 0.0 reduce-scatter.3.cloned.1.call-update
  232.7 0.3 reduce-scatter.5.cloned.1.call-start
  233.0 8.2 %multiply_convert_fusion = bf16[4,640,1024]{2,1,0:T(8,128)(2,1)S(1)} fusion(f32[4,640]{1,0:T(4,128)S(1)} %mul.52, bf16[4,640,768]{2,1,0:T(8,128)(2,1)} %multiply_convert_fusion.2, bf16[4,768,2048]{2,1,0:T(8,128)(2,1)} %param.11), kind=kOutput, calls=%fused_computation.2 | convolution fusion | flops 4031774720 | bytes 15476736 | tf_op jit(solution)/shard_map/ekf,efd->ekd/dot_general | solution.py:62
  241.2 4.0 copy.83
  245.2 5.8 bitcast_convert_fusion
  251.0 0.0 reduce-scatter.5.cloned.1.call-update
  251.1 0.5 broadcast_multiply_fusion
  251.6 164.2 %reduce-scatter.3.cloned.1.call-done = bf16[128,1024]{1,0:T(8,128)(2,1)} async-done(((bf16[4096,1024]{1,0:T(8,128)(2,1)}), bf16[128,1024]{1,0:T(8,128)(2,1)}) %reduce-scatter.3.cloned.1.call-update) | async-done | bytes 262160 | tf_op jit(solution)/shard_map/reduce_scatter | solution.py:66
  415.8 186.3 %reduce-scatter.5.cloned.1.call-done = bf16[128,1024]{1,0:T(8,128)(2,1)} async-done(((bf16[4096,1024]{1,0:T(8,128)(2,1)}), bf16[128,1024]{1,0:T(8,128)(2,1)}) %reduce-scatter.5.cloned.1.call-update) | async-done | bytes 262160 | tf_op jit(solution)/shard_map/reduce_scatter | solution.py:66
  602.1 1.9 pad_maximum_fusion
  (10 shorter events, 0.2 us)
Async XLA Ops:
  7.2 85.4 %all-gather.7.cloned.1.call-start = ((), (), s32[]{:S(2)}) async-start(), calls=%async_computation.3 | async-start | bytes 8650752 | tf_op jit(solution)/shard_map/all_gather | solution.py:30
  9.1 162.7 %all-gather.5.cloned.1.call-start = ((), (), s32[]{:S(2)}) async-start(), calls=%async_computation.2 | async-start | bytes 8650752 | tf_op jit(solution)/shard_map/all_gather | solution.py:30
  9.8 406.0 %reduce-scatter.3.cloned.1.call-start = ((), (), s32[]{:S(2)}) async-start(), calls=%async_computation.4 | async-start | bytes 8650752 | tf_op jit(solution)/shard_map/reduce_scatter | solution.py:66
  181.9 2.4 copy-start
  232.7 369.4 %reduce-scatter.5.cloned.1.call-start = ((), (), s32[]{:S(2)}) async-start(), calls=%async_computation.5 | async-start | bytes 8650752 | tf_op jit(solution)/shard_map/reduce_scatter | solution.py:66
Sparse Core Ops, SparseCore 0:
  11.5 80.9 all-gather.6
  95.5 76.1 all-gather.4
  232.8 182.9 reduce-scatter.2
  418.0 184.0 reduce-scatter.4
